TPU v7x, 32 devices: a whole 2x2x4 slice. The times are simulated.
32 devices in a mesh: dp: 4 (over z), krow: 8 (over y, x, core).
Axes of the slice: x: 2, y: 2, z: 4, core: 2. Of those that a mesh axis runs over, the one named last changes fastest.
Arguments:
- tokens: bfloat16 [12, 2048, 768], P('dp', 'krow'), may hold values from -6 to 6
- lengths: int32 [12], P('dp'), may hold values from 65 to 2048, as said below
- attn_gain: float32 [768], replicated, may hold values from 0.5 to 1.5
- attn_bias: float32 [768], replicated, may hold values from -1 to 1
- query_weight: bfloat16 [768, 768], replicated, may hold values from -0.4375 to 0.4375
- key_weight: bfloat16 [768, 768], replicated, may hold values from -0.21875 to 0.21875
- value_weight: bfloat16 [768, 768], replicated, may hold values from -0.21875 to 0.21875
- out_weight: bfloat16 [768, 768], replicated, may hold values from -3.5 to 3.5
- compress: bfloat16 [256, 2048], P('krow'), may hold values from -0.125 to 0.125
- ffn_gain: float32 [768], replicated, may hold values from 0.5 to 1.5
- ffn_bias: float32 [768], replicated, may hold values from -1 to 1
- up_weight: bfloat16 [768, 3072], replicated, may hold values from -0.21875 to 0.21875
- down_weight: bfloat16 [3072, 768], replicated, may hold values from -0.109375 to 0.109375
- cotangent: bfloat16 [12, 2048, 768], P('dp', 'krow'), may hold values from -6 to 6
Outputs:
- block_out: bfloat16 [12, 2048, 768], P('dp', 'krow')
- tokens_grad: bfloat16 [12, 2048, 768], P('dp', 'krow')
- attn_gain_grad: float32 [768], replicated
- attn_bias_grad: float32 [768], replicated
- query_weight_grad: float32 [768, 768], replicated
- key_weight_grad: float32 [768, 768], replicated
- value_weight_grad: float32 [768, 768], replicated
- out_weight_grad: float32 [768, 768], replicated
- compress_grad: float32 [256, 2048], P('krow')
- ffn_gain_grad: float32 [768], replicated
- ffn_bias_grad: float32 [768], replicated
- up_weight_grad: float32 [768, 3072], replicated
- down_weight_grad: float32 [3072, 768], replicated
- grad_norm: float32 [], replicated
Inputs may be any that keep to these rules, and one draw needn't show every extreme that they name: `lengths`: at least one sequence is 2048 positions long; positions at or past a sequence's length are padding.
All inputs are finite; a program needn't handle non-finite values.
Results may differ from a plain program's by a relative error of at most 0.019.
Values may be sent and summed in bfloat16 or wider, within the bound.
No kernel may reach another device: no remote copies, remote signals or barrier semaphores. Data moves between devices by JAX's collectives and lax.ppermute only.
A program may use at most 256 MiB of HBM per device.

v0:
```python
import jax
import jax.numpy as jnp
from jax import lax
from jax.sharding import PartitionSpec as P

D = 768
HEADS = 12
HEAD_DIM = 64
FF = 3072
EPSILON = 1e-05


def joined(value, axis, combine):
    everything = jax.tree.map(lambda part: lax.all_gather(part, axis), value)
    first = jax.tree.map(lambda part: part[0], everything)

    def hop(k, so_far):
        return combine(so_far, jax.tree.map(lambda part: part[k], everything))

    return lax.fori_loop(1, lax.axis_size(axis), hop, first)


def normalize(values, scale_vec, shift_vec):
    centred = values - jnp.mean(values, axis=-1, keepdims=True)
    spread = jnp.mean(centred * centred, axis=-1, keepdims=True)
    return centred * lax.rsqrt(spread + EPSILON) * scale_vec + shift_vec


def activate(hidden):
    return jax.nn.gelu(hidden, approximate=False)


def product(left_side, right_side):
    return jnp.dot(left_side, right_side, preferred_element_type=jnp.float32)


def product_back(grad_rows, weight):
    return lax.dot_general(
        grad_rows,
        weight,
        (((grad_rows.ndim - 1,), (1,)), ((), ())),
        preferred_element_type=jnp.float32,
    )


def contract_rows(left_side, right_side):
    left_flat = left_side.reshape(-1, left_side.shape[-1])
    right_flat = right_side.reshape(-1, right_side.shape[-1])
    return lax.dot_general(
        left_flat, right_flat, (((0,), (0,)), ((), ())), preferred_element_type=jnp.float32
    )


def combine_stats(left_pair, right_pair):
    largest = jnp.maximum(left_pair[0], right_pair[0])
    summed = left_pair[1] * jnp.exp(left_pair[0] - largest) + right_pair[1] * jnp.exp(
        right_pair[0] - largest
    )
    return (largest, summed)


def split_heads(matrix):
    return matrix.reshape(matrix.shape[0], matrix.shape[1], HEADS, HEAD_DIM)


def attend_scores(query_rows, key_rows):
    return jnp.einsum(
        "sthd,sjhd->shjt",
        split_heads(query_rows),
        split_heads(key_rows),
        preferred_element_type=jnp.float32,
    ) * HEAD_DIM ** (-0.5)


def mix_values(weights, value_rows):
    mixed_heads = jnp.einsum(
        "shjt,sjhd->sthd", weights, split_heads(value_rows), preferred_element_type=jnp.float32
    )
    return mixed_heads.reshape(mixed_heads.shape[0], mixed_heads.shape[1], D)


def head_sum(weights, rows):
    summed = jnp.einsum(
        "shjt,sthd->sjhd", weights, split_heads(rows), preferred_element_type=jnp.float32
    )
    return summed.reshape(summed.shape[0], summed.shape[1], D)


def prob_grads(grad_rows, value_rows):
    return jnp.einsum(
        "sthd,sjhd->shjt",
        split_heads(grad_rows),
        split_heads(value_rows),
        preferred_element_type=jnp.float32,
    )


def score_grads(attn_probs, grad_probs, row_dot):
    return (attn_probs * (grad_probs - row_dot[:, :, None, :])).astype(jnp.bfloat16)


def local(
    tokens,
    lengths,
    attn_gain,
    attn_bias,
    query_weight,
    key_weight,
    value_weight,
    out_weight,
    compress,
    ffn_gain,
    ffn_bias,
    up_weight,
    down_weight,
    cotangent,
):
    local_len = tokens.shape[1]
    full_len = local_len * lax.axis_size("krow")
    score_scale = HEAD_DIM ** (-0.5)
    positions = jnp.arange(full_len, dtype=jnp.int32)
    valid_mask = positions[None, :] < lengths[:, None]
    masked = compress[None, :, :] * valid_mask.astype(jnp.bfloat16)[:, None, :]
    inputs = tokens.astype(jnp.float32)
    normed, normed_back = jax.vjp(normalize, inputs, attn_gain, attn_bias)
    normed_low = normed.astype(jnp.bfloat16)
    queries = product(normed_low, query_weight).astype(jnp.bfloat16)
    full_normed, full_queries = (
        lax.all_gather(normed_low, "krow", axis=1, tiled=True),
        lax.all_gather(queries, "krow", axis=1, tiled=True),
    )
    summary = jnp.einsum(
        "sjt,std->sjd", masked, full_normed, preferred_element_type=jnp.float32
    ).astype(jnp.bfloat16)
    key_rows = product(summary, key_weight).astype(jnp.bfloat16)
    value_rows = product(summary, value_weight).astype(jnp.bfloat16)
    scores = attend_scores(full_queries, key_rows)
    local_top = jnp.max(scores, axis=2)
    local_sum = jnp.sum(jnp.exp(scores - local_top[:, :, None, :]), axis=2)
    largest, denominator = joined((local_top, local_sum), "krow", combine_stats)
    attn_probs = jnp.exp(scores - largest[:, :, None, :]) / denominator[:, :, None, :]
    mixed_rows = lax.psum_scatter(
        mix_values(attn_probs.astype(jnp.bfloat16), value_rows),
        "krow",
        scatter_dimension=1,
        tiled=True,
    )
    mixed_low = mixed_rows.astype(jnp.bfloat16)
    attended = inputs + product(mixed_low, out_weight)
    lifted, lifted_back = jax.vjp(normalize, attended, ffn_gain, ffn_bias)
    lifted_low = lifted.astype(jnp.bfloat16)
    active, active_back = jax.vjp(activate, product(lifted_low, up_weight))
    active_low = active.astype(jnp.bfloat16)
    block_out = (attended + product(active_low, down_weight)).astype(jnp.bfloat16)
    down_weight_grad = contract_rows(active_low, cotangent)
    (grad_hidden,) = active_back(product_back(cotangent, down_weight))
    grad_hidden = grad_hidden.astype(jnp.bfloat16)
    up_weight_grad = contract_rows(lifted_low, grad_hidden)
    lifted_input_grad, ffn_gain_grad, ffn_bias_grad = lifted_back(
        product_back(grad_hidden, up_weight)
    )
    grad_attended = cotangent.astype(jnp.float32) + lifted_input_grad
    grad_branch = grad_attended.astype(jnp.bfloat16)
    out_weight_grad = contract_rows(mixed_low, grad_branch)
    grad_mixed = product_back(grad_branch, out_weight).astype(jnp.bfloat16)
    full_grad_mixed = lax.all_gather(grad_mixed, "krow", axis=1, tiled=True)
    attn_probs = (
        jnp.exp(attend_scores(full_queries, key_rows) - largest[:, :, None, :])
        / denominator[:, :, None, :]
    )
    grad_probs = prob_grads(full_grad_mixed, value_rows)
    row_dot = lax.psum(jnp.sum(attn_probs * grad_probs, axis=2), "krow")
    grad_scores = score_grads(attn_probs, grad_probs, row_dot)
    grad_values = head_sum(attn_probs.astype(jnp.bfloat16), full_grad_mixed).astype(jnp.bfloat16)
    grad_keys = (head_sum(grad_scores, full_queries) * score_scale).astype(jnp.bfloat16)
    query_part = mix_values(grad_scores, key_rows) * score_scale
    grad_queries = lax.psum_scatter(
        query_part.astype(jnp.bfloat16), "krow", scatter_dimension=1, tiled=True
    )
    grad_summary = (
        product_back(grad_keys, key_weight) + product_back(grad_values, value_weight)
    ).astype(jnp.bfloat16)
    normed_part = jnp.einsum(
        "sjt,sjd->std", masked, grad_summary, preferred_element_type=jnp.float32
    )
    normed_extra = lax.psum_scatter(
        normed_part.astype(jnp.bfloat16), "krow", scatter_dimension=1, tiled=True
    ).astype(jnp.float32)
    compress_terms = jnp.einsum(
        "sjd,std->sjt", grad_summary, full_normed, preferred_element_type=jnp.float32
    )
    compress_local = jnp.sum(compress_terms * valid_mask.astype(jnp.float32)[:, None, :], axis=0)
    compress_grad = lax.psum(compress_local.astype(jnp.bfloat16), "dp").astype(jnp.float32)
    query_weight_grad = contract_rows(normed_low, grad_queries)
    key_weight_grad = contract_rows(summary, grad_keys)
    value_weight_grad = contract_rows(summary, grad_values)
    grad_normed = product_back(grad_queries, query_weight) + normed_extra
    normed_input_grad, attn_gain_grad, attn_bias_grad = normed_back(grad_normed)
    tokens_grad = (grad_attended + normed_input_grad).astype(jnp.bfloat16)
    norm_grads = jnp.stack([attn_gain_grad, attn_bias_grad, ffn_gain_grad, ffn_bias_grad])
    shards = (
        lax.psum_scatter(
            query_weight_grad.reshape(-1), ("dp", "krow"), scatter_dimension=0, tiled=True
        ),
        lax.psum_scatter(
            key_weight_grad.reshape(-1), ("dp", "krow"), scatter_dimension=0, tiled=True
        ),
        lax.psum_scatter(
            value_weight_grad.reshape(-1), ("dp", "krow"), scatter_dimension=0, tiled=True
        ),
        lax.psum_scatter(
            out_weight_grad.reshape(-1), ("dp", "krow"), scatter_dimension=0, tiled=True
        ),
        lax.psum_scatter(
            up_weight_grad.reshape(-1), ("dp", "krow"), scatter_dimension=0, tiled=True
        ),
        lax.psum_scatter(
            down_weight_grad.reshape(-1), ("dp", "krow"), scatter_dimension=0, tiled=True
        ),
        lax.psum_scatter(norm_grads.reshape(-1), ("dp", "krow"), scatter_dimension=0, tiled=True),
    )
    gathered = (
        lax.all_gather(shards[0].astype(jnp.bfloat16), ("dp", "krow"), axis=0, tiled=True).astype(
            jnp.float32
        ),
        lax.all_gather(shards[1].astype(jnp.bfloat16), ("dp", "krow"), axis=0, tiled=True).astype(
            jnp.float32
        ),
        lax.all_gather(shards[2].astype(jnp.bfloat16), ("dp", "krow"), axis=0, tiled=True).astype(
            jnp.float32
        ),
        lax.all_gather(shards[3].astype(jnp.bfloat16), ("dp", "krow"), axis=0, tiled=True).astype(
            jnp.float32
        ),
        lax.all_gather(shards[4].astype(jnp.bfloat16), ("dp", "krow"), axis=0, tiled=True).astype(
            jnp.float32
        ),
        lax.all_gather(shards[5].astype(jnp.bfloat16), ("dp", "krow"), axis=0, tiled=True).astype(
            jnp.float32
        ),
        lax.all_gather(shards[6].astype(jnp.bfloat16), ("dp", "krow"), axis=0, tiled=True).astype(
            jnp.float32
        ),
    )
    grad_norm = jnp.sqrt(sum((jnp.sum(member * member) for member in gathered)))
    norm_block = gathered[6].reshape(4, D)
    return (
        block_out,
        tokens_grad,
        norm_block[0],
        norm_block[1],
        gathered[0].reshape(D, D),
        gathered[1].reshape(D, D),
        gathered[2].reshape(D, D),
        gathered[3].reshape(D, D),
        compress_grad,
        norm_block[2],
        norm_block[3],
        gathered[4].reshape(D, FF),
        gathered[5].reshape(FF, D),
        grad_norm,
    )


def solution(mesh):
    in_specs = (
        P("dp", "krow", None),
        P("dp"),
        P(),
        P(),
        P(),
        P(),
        P(),
        P(),
        P("krow", None),
        P(),
        P(),
        P(),
        P(),
        P("dp", "krow", None),
    )
    out_specs = (
        P("dp", "krow", None),
        P("dp", "krow", None),
        P(),
        P(),
        P(),
        P(),
        P(),
        P(),
        P("krow", None),
        P(),
        P(),
        P(),
        P(),
        P(),
    )
    return jax.shard_map(local, mesh=mesh, in_specs=in_specs, out_specs=out_specs, check_vma=False)
```

profile of v0, /device:TPU:0, one launch (start us, length us, event | category | flops | bytes accessed | tf_op | source)
XLA Modules:
  0.0 1617.0 jit_solution(11979326768688022540)
XLA Ops:
  18.9 57.5 %all-gather.14.cloned.1.call-done = bf16[3,2048,768]{2,1,0:T(8,128)(2,1)} async-done(((bf16[3,256,768]{2,1,0:T(8,128)(2,1)}), bf16[3,2048,768]{2,1,0:T(8,128)(2,1)}) %all-gather.14.cloned.1.call-update) | async-done | bytes 9437200 | tf_op jit(solution)/shard_map/all_gather | solution.py:129
  82.5 55.2 %all-gather.16.cloned.1.call-done = bf16[3,2048,768]{2,1,0:T(8,128)(2,1)} async-done(((bf16[3,256,768]{2,1,0:T(8,128)(2,1)}), bf16[3,2048,768]{2,1,0:T(8,128)(2,1)}) %all-gather.16.cloned.1.call-update) | async-done | bytes 9437200 | tf_op jit(solution)/shard_map/all_gather | solution.py:130
  137.7 12.6 copy.54
  168.5 24.5 %all-gather.32.cloned.1.call-done = f32[24,12,2048]{2,1,0:T(8,128)} async-done(((f32[3,12,2048]{2,1,0:T(8,128)}), f32[24,12,2048]{2,1,0:T(8,128)}) %all-gather.32.cloned.1.call-update) | async-done | bytes 2359312 | tf_op jit(solution)/shard_map/all_gather | solution.py:14
  194.0 33.6 %all-gather.34.cloned.1.call-done = f32[24,12,2048]{2,1,0:T(8,128)} async-done(((f32[3,12,2048]{2,1,0:T(8,128)}), f32[24,12,2048]{2,1,0:T(8,128)}) %all-gather.34.cloned.1.call-update) | async-done | bytes 2359312 | tf_op jit(solution)/shard_map/all_gather | solution.py:14
  228.7 10.4 while.17
  239.0 12.8 fusion.28
  251.9 126.2 %reduce-scatter.4.cloned.1.call-done = f32[3,256,768]{1,2,0:T(8,128)} async-done(((f32[3,2048,768]{1,2,0:T(8,128)}), f32[3,256,768]{1,2,0:T(8,128)}) %reduce-scatter.4.cloned.1.call-update) | async-done | bytes 2359312 | tf_op jit(solution)/shard_map/reduce_scatter | solution.py:142
  390.6 22.6 %multiply_convert_fusion.2 = (bf16[3,256,3072]{2,1,0:T(8,128)(2,1)}, f32[3,256,3072]{2,1,0:T(8,128)}) fusion(f32[3,256,3072]{2,1,0:T(8,128)S(1)} %get-tuple-element.190, u8[256,3072]{1,0:T(8,128)(4,1)S(1)} %get-tuple-element.150, u8[256,3072]{1,0:T(8,128)(4,1)S(1)} %get-tuple-element.149), kind=kLoop, calls=%fused_computation.18 | loop fusion | flops 165150720 | bytes 25165824 | tf_op jit(solution)/shard_map/convert_element_type | solution.py:153
  413.1 11.2 add_convert_fusion
  438.5 58.9 %all-gather.18.cloned.1.call-done = bf16[3,2048,768]{2,1,0:T(8,128)(2,1)} async-done(((bf16[3,256,768]{2,1,0:T(8,128)(2,1)}), bf16[3,2048,768]{2,1,0:T(8,128)(2,1)}) %all-gather.18.cloned.1.call-update) | async-done | bytes 9437200 | tf_op jit(solution)/shard_map/all_gather | solution.py:166
  497.4 12.7 copy.58
  510.1 12.5 multiply_reduce_fusion.2
  522.7 54.2 %all-reduce.13.cloned.1.call-done = f32[3,12,2048]{2,1,0:T(8,128)} async-done(((f32[3,12,2048]{2,1,0:T(8,128)}), f32[3,12,2048]{2,1,0:T(8,128)}) %all-reduce.13.cloned.1.call-update) | async-done | bytes 294928 | tf_op jit(solution)/shard_map/psum | solution.py:172
  590.1 12.7 copy.61
  659.8 10.7 reshape.240
  688.1 71.3 %reduce-scatter.8.cloned.1.call-done = bf16[3,256,768]{2,1,0:T(8,128)(2,1)} async-done(((bf16[3,2048,768]{2,1,0:T(8,128)(2,1)}), bf16[3,256,768]{2,1,0:T(8,128)(2,1)}) %reduce-scatter.8.cloned.1.call-update) | async-done | bytes 1179664 | tf_op jit(solution)/shard_map/reduce_scatter | solution.py:186
  772.3 456.3 %all-reduce.16 = (bf16[3072]{0:T(1024)(128)(2,1)S(1)}, bf16[589824]{0:T(1024)(128)(2,1)}, bf16[589824]{0:T(1024)(128)(2,1)}, bf16[589824]{0:T(1024)(128)(2,1)}, ...) all-reduce(f32[3072]{0:T(1024)S(1)} %reshape.229, ...), channel_id=7, replica_groups=mesh['dp'=4,'krow'=8] {'dp','krow'}, use_global_device_ids=true, to_apply=%region_21.0.clone | all-reduce | flops 7080960 | bytes 42485760
  1248.9 38.8 %all-reduce = bf16[3072]{0:T(1024)(128)(2,1)S(1)} all-reduce(bf16[3072]{0:T(1024)(128)(2,1)S(1)} %dynamic-update-slice), channel_id=1, replica_groups=mesh['dp'=4,'krow'=8] {'dp','krow'}, use_global_device_ids=true, to_apply=%add | all-reduce | flops 3072 | bytes 12288
  1295.3 43.0 %all-gather.22.cloned.1.call-done = bf16[589824]{0:T(1024)(128)(2,1)} async-done(((bf16[18432]{0:T(1024)(128)(2,1)}), bf16[589824]{0:T(1024)(128)(2,1)}) %all-gather.22.cloned.1.call-update) | async-done | bytes 1179664 | tf_op jit(solution)/shard_map/all_gather | solution.py:226
  1342.0 52.5 %all-gather.24.cloned.1.call-done = bf16[589824]{0:T(1024)(128)(2,1)} async-done(((bf16[18432]{0:T(1024)(128)(2,1)}), bf16[589824]{0:T(1024)(128)(2,1)}) %all-gather.24.cloned.1.call-update) | async-done | bytes 1179664 | tf_op jit(solution)/shard_map/all_gather | solution.py:229
  1397.7 53.6 %all-gather.26.cloned.1.call-done = bf16[589824]{0:T(1024)(128)(2,1)} async-done(((bf16[18432]{0:T(1024)(128)(2,1)}), bf16[589824]{0:T(1024)(128)(2,1)}) %all-gather.26.cloned.1.call-update) | async-done | bytes 1179664 | tf_op jit(solution)/shard_map/all_gather | solution.py:232
  1463.9 53.7 %all-gather.28.cloned.1.call-done = bf16[2359296]{0:T(1024)(128)(2,1)} async-done(((bf16[73728]{0:T(1024)(128)(2,1)}), bf16[2359296]{0:T(1024)(128)(2,1)}) %all-gather.28.cloned.1.call-update) | async-done | bytes 4718608 | tf_op jit(solution)/shard_map/all_gather | solution.py:235
  1523.3 60.5 %all-gather.30.cloned.1.call-done = bf16[2359296]{0:T(1024)(128)(2,1)} async-done(((bf16[73728]{0:T(1024)(128)(2,1)}), bf16[2359296]{0:T(1024)(128)(2,1)}) %all-gather.30.cloned.1.call-update) | async-done | bytes 4718608 | tf_op jit(solution)/shard_map/all_gather | solution.py:238
  (237 shorter events, 248.4 us)
Async XLA Ops:
  7.2 370.9 %copy-start = (bf16[768,768]{1,0:T(8,128)(2,1)S(1)}, bf16[768,768]{1,0:T(8,128)(2,1)}, u32[]{:S(2)}) copy-start(bf16[768,768]{1,0:T(8,128)(2,1)} %param.23) | copy-start | bytes 3538948
  7.2 69.2 %all-gather.14.cloned.1.call-start = ((), (), s32[]{:S(2)}) async-start(), calls=%async_computation.3 | async-start | bytes 10616832 | tf_op jit(solution)/shard_map/all_gather | solution.py:129
  14.7 123.0 %all-gather.16.cloned.1.call-start = ((), (), s32[]{:S(2)}) async-start(), calls=%async_computation.4 | async-start | bytes 10616832 | tf_op jit(solution)/shard_map/all_gather | solution.py:130
  18.2 174.8 %all-gather.32.cloned.1.call-start = ((), (), s32[]{:S(2)}) async-start(), calls=%async_computation.17 | async-start | bytes 3538944 | tf_op jit(solution)/shard_map/all_gather | solution.py:14
  81.9 86.0 %copy-start.7 = (bf16[3,32,768]{2,1,0:T(8,128)(2,1)}, bf16[3,32,768]{2,1,0:T(8,128)(2,1)S(1)}, u32[]{:S(2)}) copy-start(bf16[3,32,768]{2,1,0:T(8,128)(2,1)S(1)} %convolution_convert_fusion.3) | copy-start | bytes 442372
  160.5 67.1 %all-gather.34.cloned.1.call-start = ((), (), s32[]{:S(2)}) async-start(), calls=%async_computation.18 | async-start | bytes 3538944 | tf_op jit(solution)/shard_map/all_gather | solution.py:14
  167.3 210.8 %reduce-scatter.4.cloned.1.call-start = ((), (), s32[]{:S(2)}) async-start(), calls=%async_computation.5 | async-start | bytes 21233664 | tf_op jit(solution)/shard_map/reduce_scatter | solution.py:142
  251.8 126.3 %copy-start.3 = (bf16[3,256,768]{2,1,0:T(8,128)(2,1)S(1)}, bf16[3,256,768]{2,1,0:T(8,128)(2,1)}, u32[]{:S(2)}) copy-start(bf16[3,256,768]{2,1,0:T(8,128)(2,1)} %param.16) | copy-start | bytes 3538948
  251.9 129.6 %copy-start.30 = (f32[768]{0:T(1024)S(1)}, f32[768]{0:T(1024)}, u32[]{:S(2)}) copy-start(f32[768]{0:T(1024)} %param.25) | copy-start | bytes 9220
  251.9 129.6 %copy-start.31 = (f32[768]{0:T(1024)S(1)}, f32[768]{0:T(1024)}, u32[]{:S(2)}) copy-start(f32[768]{0:T(1024)} %param.26) | copy-start | bytes 9220
  251.9 245.5 %all-gather.18.cloned.1.call-start = ((), (), s32[]{:S(2)}) async-start(), calls=%async_computation.6 | async-start | bytes 10616832 | tf_op jit(solution)/shard_map/all_gather | solution.py:166
  438.4 138.5 %all-reduce.13.cloned.1.call-start = ((), (), s32[]{:S(2)}) async-start(), calls=%async_computation.7 | async-start | bytes 786432 | tf_op jit(solution)/shard_map/psum | solution.py:172
  522.7 165.4 %reduce-scatter.6.cloned.1.call-start = ((), (), s32[]{:S(2)}) async-start(), calls=%async_computation.8 | async-start | bytes 10616832 | tf_op jit(solution)/shard_map/reduce_scatter | solution.py:177
  602.8 156.6 %reduce-scatter.8.cloned.1.call-start = ((), (), s32[]{:S(2)}) async-start(), calls=%async_computation.9 | async-start | bytes 10616832 | tf_op jit(solution)/shard_map/reduce_scatter | solution.py:186
  630.1 616.9 %all-reduce.15.cloned.1.call-start = ((), (), s32[]{:S(2)}) async-start(), calls=%async_computation.14 | async-start | bytes 262144 | tf_op jit(solution)/shard_map/psum | solution.py:193
  680.8 78.7 %copy-start.33 = (f32[3,256]{1,0:T(4,128)S(1)}, f32[3,256]{1,0:T(4,128)}, u32[]{:S(2)}) copy-start(f32[3,256]{1,0:T(4,128)} %copy-done.32) | copy-start | bytes 9220
  680.8 78.7 %copy-start.38 = (f32[768]{0:T(1024)S(1)}, f32[768]{0:T(1024)}, u32[]{:S(2)}) copy-start(f32[768]{0:T(1024)} %param.18) | copy-start | bytes 9220
  688.1 604.7 %all-gather.20.cloned.1.call-start = ((), (), s32[]{:S(2)}) async-start(), calls=%async_computation.10 | async-start | bytes 1216512 | tf_op jit(solution)/shard_map/all_gather | solution.py:223
  1230.0 108.2 %all-gather.22.cloned.1.call-start = ((), (), s32[]{:S(2)}) async-start(), calls=%async_computation.11 | async-start | bytes 1216512 | tf_op jit(solution)/shard_map/all_gather | solution.py:226
  1231.5 163.1 %all-gather.24.cloned.1.call-start = ((), (), s32[]{:S(2)}) async-start(), calls=%async_computation.12 | async-start | bytes 1216512 | tf_op jit(solution)/shard_map/all_gather | solution.py:229
  1232.9 218.4 %all-gather.26.cloned.1.call-start = ((), (), s32[]{:S(2)}) async-start(), calls=%async_computation.13 | async-start | bytes 1216512 | tf_op jit(solution)/shard_map/all_gather | solution.py:232
  1234.4 283.2 %all-gather.28.cloned.1.call-start = ((), (), s32[]{:S(2)}) async-start(), calls=%async_computation.15 | async-start | bytes 4866048 | tf_op jit(solution)/shard_map/all_gather | solution.py:235
  1236.0 347.8 %all-gather.30.cloned.1.call-start = ((), (), s32[]{:S(2)}) async-start(), calls=%async_computation.16 | async-start | bytes 4866048 | tf_op jit(solution)/shard_map/all_gather | solution.py:238
  1342.0 117.9 %copy-start.13 = (bf16[589824]{0:T(1024)(128)(2,1)S(1)}, bf16[589824]{0:T(1024)(128)(2,1)}, u32[]{:S(2)}) copy-start(bf16[589824]{0:T(1024)(128)(2,1)} %all-gather.22.cloned.1.call-done) | copy-start | bytes 3538948
  (46 other events, 927.4 us)
Sparse Core Ops, SparseCore 0:
  14.8 61.5 all-gather.13
  78.9 58.8 all-gather.15
  160.6 32.3 all-gather.31
  195.3 32.3 all-gather.33
  252.0 126.0 reduce-scatter.3
  438.6 58.8 all-gather.17
  522.8 54.1 all-reduce.12
  603.0 75.7 reduce-scatter.5
  682.9 76.5 reduce-scatter.7
  762.2 34.4 all-reduce.14
  1230.1 51.9 all-gather.19
  1285.3 52.9 all-gather.21
  1341.5 52.9 all-gather.23
  1398.3 52.9 all-gather.25
  1455.0 62.5 all-gather.27
  1521.4 62.4 all-gather.29
where the time goes:
time: 1630 us; the launch traced here: 1620 us
  waiting for transfers between devices  745 us (46%)
  blocking collectives  495 us (30%)
  matrix products  154 us (9%)
  local copies, waits for them, and re-layouts  116 us (7%)
  other arithmetic  84.4 us (5%)
  between operations  20.6 us (1%)
    unnamed x2, blocking collectives  495 us
    reduce_scatter x1, waiting for transfers between devices, local(): lax.psum_scatter(mix_values(attn_probs.astype(jnp.bfloat16), value_rows),...  126 us
    reduce_scatter x1, waiting for transfers between devices, local(): lax.psum_scatter(normed_part.astype(jnp.bfloat16), 'krow', scatter_dimens...  71.3 us
    all_gather x1, waiting for transfers between devices, local(): lax.all_gather(shards[5].astype(jnp.bfloat16), ('dp', 'krow'), axis=0, ti...  60.5 us
    all_gather x1, waiting for transfers between devices, local(): full_grad_mixed = lax.all_gather(grad_mixed, 'krow', axis=1, tiled=True)  58.9 us
    all_gather x2, waiting for transfers between devices, joined(): everything = jax.tree.map(lambda part: lax.all_gather(part, axis), value)  58.1 us
    all_gather x1, waiting for transfers between devices, local(): lax.all_gather(normed_low, 'krow', axis=1, tiled=True)  57.5 us
    all_gather x1, waiting for transfers between devices, local(): lax.all_gather(queries, 'krow', axis=1, tiled=True)  55.2 us
  transfers between devices with their start and end apart: 16, of which 13 were waited for; matrix products, arithmetic and copies ran while one was open for 10% of the time, Pallas kernels for 0%

commit v1 on v0

--- a/solution.py
+++ b/solution.py
@@ -163,7 +163,12 @@
     grad_branch = grad_attended.astype(jnp.bfloat16)
     out_weight_grad = contract_rows(mixed_low, grad_branch)
     grad_mixed = product_back(grad_branch, out_weight).astype(jnp.bfloat16)
-    full_grad_mixed = lax.all_gather(grad_mixed, "krow", axis=1, tiled=True)
+    ring = [grad_mixed]
+    for hop_ in range(7):
+        ring.append(lax.ppermute(ring[-1], "krow", [(dev, (dev + 1) % 8) for dev in range(8)]))
+    full_grad_mixed = jnp.roll(
+        jnp.concatenate(ring[::-1], axis=1), (lax.axis_index("krow") + 1) * ring[0].shape[1], axis=1
+    )
     attn_probs = (
         jnp.exp(attend_scores(full_queries, key_rows) - largest[:, :, None, :])
         / denominator[:, :, None, :]

time: 1630 us -> 1720 us (1.055)
  waiting for transfers between devices: 745 us -> 810 us
  local copies, waits for them, and re-layouts: 116 us -> 149 us
    ppermute x0 -> x7, waiting for transfers between devices: none -> 116 us  [local(): lax.ppermute(ring[-1], 'krow', [(dev, (dev + 1) % 8) for dev in range(8)])]
    all_gather x1 -> x0, waiting for transfers between devices: 58.9 us -> none  [local(): full_grad_mixed = lax.all_gather(grad_mixed, 'krow', axis=1, tiled=True)]
    all_gather x1, waiting for transfers between devices: 43 us -> 0.01 us  [local(): lax.all_gather(shards[1].astype(jnp.bfloat16), ('dp', 'krow'), axis=0, ti...]
    all_gather x1, waiting for transfers between devices: 0.01 us -> 42.1 us  [local(): lax.all_gather(shards[0].astype(jnp.bfloat16), ('dp', 'krow'), axis=0, ti...]
    unnamed x118 -> x151, local copies, waits for them, and re-layouts: 20.7 us -> 43.6 us
    dynamic_slice x0 -> x2, local copies, waits for them, and re-layouts: none -> 20.8 us  [local(): jnp.roll(jnp.concatenate(ring[::-1], axis=1), (lax.axis_index('krow') + 1...]
  transfers between devices with their start and end apart: 16 -> 22, of which waited for: 13 -> 19; matrix products, arithmetic and copies ran while one was open for 10% -> 9% of each run, Pallas kernels for 0% -> 0%
where the time goes in v1:
time: 1720 us; the launch traced here: 1710 us
  waiting for transfers between devices  810 us (47%)
  blocking collectives  496 us (29%)
  matrix products  151 us (9%)
  local copies, waits for them, and re-layouts  149 us (9%)
  other arithmetic  86 us (5%)
  between operations  20.6 us (1%)
    unnamed x2, blocking collectives  496 us
    reduce_scatter x1, waiting for transfers between devices, local(): lax.psum_scatter(mix_values(attn_probs.astype(jnp.bfloat16), value_rows),...  126 us
    ppermute x7, waiting for transfers between devices, local(): lax.ppermute(ring[-1], 'krow', [(dev, (dev + 1) % 8) for dev in range(8)])  116 us
    reduce_scatter x1, waiting for transfers between devices, local(): lax.psum_scatter(normed_part.astype(jnp.bfloat16), 'krow', scatter_dimens...  72.9 us
    all_gather x2, waiting for transfers between devices, joined(): everything = jax.tree.map(lambda part: lax.all_gather(part, axis), value)  64.4 us
    all_gather x1, waiting for transfers between devices, local(): lax.all_gather(shards[5].astype(jnp.bfloat16), ('dp', 'krow'), axis=0, ti...  60.5 us
    all_gather x1, waiting for transfers between devices, local(): lax.all_gather(normed_low, 'krow', axis=1, tiled=True)  57.5 us
    all_gather x1, waiting for transfers between devices, local(): lax.all_gather(queries, 'krow', axis=1, tiled=True)  55.2 us
  transfers between devices with their start and end apart: 22, of which 19 were waited for; matrix products, arithmetic and copies ran while one was open for 9% of the time, Pallas kernels for 0%

profile of v1, /device:TPU:0, one launch (start us, length us, event | category | flops | bytes accessed | tf_op | source)
XLA Modules:
  0.0 1713.0 jit_solution(7572715365137227195)
XLA Ops:
  18.9 57.5 %all-gather.13.cloned.1.call-done = bf16[3,2048,768]{2,1,0:T(8,128)(2,1)} async-done(((bf16[3,256,768]{2,1,0:T(8,128)(2,1)}), bf16[3,2048,768]{2,1,0:T(8,128)(2,1)}) %all-gather.13.cloned.1.call-update) | async-done | bytes 9437200 | tf_op jit(solution)/shard_map/all_gather | solution.py:129
  82.5 55.2 %all-gather.15.cloned.1.call-done = bf16[3,2048,768]{2,1,0:T(8,128)(2,1)} async-done(((bf16[3,256,768]{2,1,0:T(8,128)(2,1)}), bf16[3,2048,768]{2,1,0:T(8,128)(2,1)}) %all-gather.15.cloned.1.call-update) | async-done | bytes 9437200 | tf_op jit(solution)/shard_map/all_gather | solution.py:130
  168.3 30.8 %all-gather.31.cloned.1.call-done = f32[24,12,2048]{2,1,0:T(8,128)} async-done(((f32[3,12,2048]{2,1,0:T(8,128)}), f32[24,12,2048]{2,1,0:T(8,128)}) %all-gather.31.cloned.1.call-update) | async-done | bytes 2359312 | tf_op jit(solution)/shard_map/all_gather | solution.py:14
  200.1 33.6 %all-gather.29.cloned.1.call-done = f32[24,12,2048]{2,1,0:T(8,128)} async-done(((f32[3,12,2048]{2,1,0:T(8,128)}), f32[24,12,2048]{2,1,0:T(8,128)}) %all-gather.29.cloned.1.call-update) | async-done | bytes 2359312 | tf_op jit(solution)/shard_map/all_gather | solution.py:14
  245.1 12.8 fusion.28
  258.0 126.2 %reduce-scatter.4.cloned.1.call-done = f32[3,256,768]{1,2,0:T(8,128)} async-done(((f32[3,2048,768]{1,2,0:T(8,128)}), f32[3,256,768]{1,2,0:T(8,128)}) %reduce-scatter.4.cloned.1.call-update) | async-done | bytes 2359312 | tf_op jit(solution)/shard_map/reduce_scatter | solution.py:142
  396.6 22.5 %multiply_convert_fusion.2 = (bf16[3,256,3072]{2,1,0:T(8,128)(2,1)}, f32[3,256,3072]{2,1,0:T(8,128)}) fusion(f32[3,256,3072]{2,1,0:T(8,128)S(1)} %get-tuple-element.190, u8[256,3072]{1,0:T(8,128)(4,1)S(1)} %get-tuple-element.150, u8[256,3072]{1,0:T(8,128)(4,1)S(1)} %get-tuple-element.149), kind=kLoop, calls=%fused_computation.18 | loop fusion | flops 165150720 | bytes 25165824 | tf_op jit(solution)/shard_map/convert_element_type | solution.py:153
  441.1 16.5 collective-permute-done
  457.6 16.5 collective-permute-done.1
  475.2 16.5 collective-permute-done.2
  492.7 16.5 collective-permute-done.3
  510.2 16.5 collective-permute-done.4
  527.8 16.6 collective-permute-done.5
  544.4 16.8 collective-permute-done.6
  592.2 12.9 copy.56
  617.8 54.2 %all-reduce.13.cloned.1.call-done = f32[3,12,2048]{2,1,0:T(8,128)} async-done(((f32[3,12,2048]{2,1,0:T(8,128)}), f32[3,12,2048]{2,1,0:T(8,128)}) %all-reduce.13.cloned.1.call-update) | async-done | bytes 294928 | tf_op jit(solution)/shard_map/psum | solution.py:177
  781.2 72.9 %reduce-scatter.8.cloned.1.call-done = bf16[3,256,768]{2,1,0:T(8,128)(2,1)} async-done(((bf16[3,2048,768]{2,1,0:T(8,128)(2,1)}), bf16[3,256,768]{2,1,0:T(8,128)(2,1)}) %reduce-scatter.8.cloned.1.call-update) | async-done | bytes 1179664 | tf_op jit(solution)/shard_map/reduce_scatter | solution.py:191
  867.6 456.1 %all-reduce.16 = (bf16[3072]{0:T(1024)(128)(2,1)}, bf16[589824]{0:T(1024)(128)(2,1)}, bf16[589824]{0:T(1024)(128)(2,1)}, bf16[589824]{0:T(1024)(128)(2,1)}, bf16...) all-reduce(f32[3072]{0:T(1024)} %reshape.229, ...), channel_id=7, replica_groups=mesh['dp'=4,'krow'=8] {'dp','krow'}, use_global_device_ids=true, to_apply=%region_21.22.clone | all-reduce | flops 7080960 | bytes 42485760
  1344.0 39.6 %all-reduce = bf16[3072]{0:T(1024)(128)(2,1)S(1)} all-reduce(bf16[3072]{0:T(1024)(128)(2,1)S(1)} %dynamic-update-slice), channel_id=1, replica_groups=mesh['dp'=4,'krow'=8] {'dp','krow'}, use_global_device_ids=true, to_apply=%add | all-reduce | flops 3072 | bytes 12288
  1392.2 42.1 %all-gather.17.cloned.1.call-done = bf16[589824]{0:T(1024)(128)(2,1)} async-done(((bf16[18432]{0:T(1024)(128)(2,1)}), bf16[589824]{0:T(1024)(128)(2,1)}) %all-gather.17.cloned.1.call-update) | async-done | bytes 1179664 | tf_op jit(solution)/shard_map/all_gather | solution.py:228
  1438.1 52.4 %all-gather.21.cloned.1.call-done = bf16[589824]{0:T(1024)(128)(2,1)} async-done(((bf16[18432]{0:T(1024)(128)(2,1)}), bf16[589824]{0:T(1024)(128)(2,1)}) %all-gather.21.cloned.1.call-update) | async-done | bytes 1179664 | tf_op jit(solution)/shard_map/all_gather | solution.py:234
  1493.7 53.6 %all-gather.23.cloned.1.call-done = bf16[589824]{0:T(1024)(128)(2,1)} async-done(((bf16[18432]{0:T(1024)(128)(2,1)}), bf16[589824]{0:T(1024)(128)(2,1)}) %all-gather.23.cloned.1.call-update) | async-done | bytes 1179664 | tf_op jit(solution)/shard_map/all_gather | solution.py:237
  1559.9 53.8 %all-gather.25.cloned.1.call-done = bf16[2359296]{0:T(1024)(128)(2,1)} async-done(((bf16[73728]{0:T(1024)(128)(2,1)}), bf16[2359296]{0:T(1024)(128)(2,1)}) %all-gather.25.cloned.1.call-update) | async-done | bytes 4718608 | tf_op jit(solution)/shard_map/all_gather | solution.py:240
  1619.4 60.5 %all-gather.27.cloned.1.call-done = bf16[2359296]{0:T(1024)(128)(2,1)} async-done(((bf16[73728]{0:T(1024)(128)(2,1)}), bf16[2359296]{0:T(1024)(128)(2,1)}) %all-gather.27.cloned.1.call-update) | async-done | bytes 4718608 | tf_op jit(solution)/shard_map/all_gather | solution.py:243
  (282 shorter events, 349.8 us)
Async XLA Ops:
  7.2 377.0 %copy-start = (bf16[768,768]{1,0:T(8,128)(2,1)S(1)}, bf16[768,768]{1,0:T(8,128)(2,1)}, u32[]{:S(2)}) copy-start(bf16[768,768]{1,0:T(8,128)(2,1)} %param.23) | copy-start | bytes 3538948
  7.2 69.2 %all-gather.13.cloned.1.call-start = ((), (), s32[]{:S(2)}) async-start(), calls=%async_computation.3 | async-start | bytes 10616832 | tf_op jit(solution)/shard_map/all_gather | solution.py:129
  14.7 123.0 %all-gather.15.cloned.1.call-start = ((), (), s32[]{:S(2)}) async-start(), calls=%async_computation.4 | async-start | bytes 10616832 | tf_op jit(solution)/shard_map/all_gather | solution.py:130
  18.2 180.9 %all-gather.31.cloned.1.call-start = ((), (), s32[]{:S(2)}) async-start(), calls=%async_computation.17 | async-start | bytes 3538944 | tf_op jit(solution)/shard_map/all_gather | solution.py:14
  166.6 67.1 %all-gather.29.cloned.1.call-start = ((), (), s32[]{:S(2)}) async-start(), calls=%async_computation.16 | async-start | bytes 3538944 | tf_op jit(solution)/shard_map/all_gather | solution.py:14
  167.2 217.0 %reduce-scatter.4.cloned.1.call-start = ((), (), s32[]{:S(2)}) async-start(), calls=%async_computation.5 | async-start | bytes 21233664 | tf_op jit(solution)/shard_map/reduce_scatter | solution.py:142
  257.9 414.0 %all-reduce.13.cloned.1.call-start = ((), (), s32[]{:S(2)}) async-start(), calls=%async_computation.6 | async-start | bytes 786432 | tf_op jit(solution)/shard_map/psum | solution.py:177
  441.0 16.6 collective-permute-start
  457.6 16.5 collective-permute-start.1
  475.2 16.5 collective-permute-start.2
  492.7 16.5 collective-permute-start.3
  510.2 16.5 collective-permute-start.4
  527.8 16.6 collective-permute-start.5
  544.4 16.8 collective-permute-start.6
  617.7 163.5 %reduce-scatter.6.cloned.1.call-start = ((), (), s32[]{:S(2)}) async-start(), calls=%async_computation.7 | async-start | bytes 10616832 | tf_op jit(solution)/shard_map/reduce_scatter | solution.py:182
  697.6 156.5 %reduce-scatter.8.cloned.1.call-start = ((), (), s32[]{:S(2)}) async-start(), calls=%async_computation.8 | async-start | bytes 10616832 | tf_op jit(solution)/shard_map/reduce_scatter | solution.py:191
  723.7 617.7 %all-reduce.15.cloned.1.call-start = ((), (), s32[]{:S(2)}) async-start(), calls=%async_computation.13 | async-start | bytes 262144 | tf_op jit(solution)/shard_map/psum | solution.py:198
  781.1 608.5 %all-gather.19.cloned.1.call-start = ((), (), s32[]{:S(2)}) async-start(), calls=%async_computation.10 | async-start | bytes 1216512 | tf_op jit(solution)/shard_map/all_gather | solution.py:231
  1325.1 109.3 %all-gather.17.cloned.1.call-start = ((), (), s32[]{:S(2)}) async-start(), calls=%async_computation.9 | async-start | bytes 1216512 | tf_op jit(solution)/shard_map/all_gather | solution.py:228
  1326.5 164.0 %all-gather.21.cloned.1.call-start = ((), (), s32[]{:S(2)}) async-start(), calls=%async_computation.11 | async-start | bytes 1216512 | tf_op jit(solution)/shard_map/all_gather | solution.py:234
  1328.0 219.4 %all-gather.23.cloned.1.call-start = ((), (), s32[]{:S(2)}) async-start(), calls=%async_computation.12 | async-start | bytes 1216512 | tf_op jit(solution)/shard_map/all_gather | solution.py:237
  1329.5 284.3 %all-gather.25.cloned.1.call-start = ((), (), s32[]{:S(2)}) async-start(), calls=%async_computation.14 | async-start | bytes 4866048 | tf_op jit(solution)/shard_map/all_gather | solution.py:240
  1331.1 348.8 %all-gather.27.cloned.1.call-start = ((), (), s32[]{:S(2)}) async-start(), calls=%async_computation.15 | async-start | bytes 4866048 | tf_op jit(solution)/shard_map/all_gather | solution.py:243
  1389.6 164.4 %copy-start.15 = (bf16[589824]{0:T(1024)(128)(2,1)S(1)}, bf16[589824]{0:T(1024)(128)(2,1)}, u32[]{:S(2)}) copy-start(bf16[589824]{0:T(1024)(128)(2,1)} %all-gather.19.cloned.1.call-done) | copy-start | bytes 3538948
  (61 other events, 1666.6 us)
Sparse Core Ops, SparseCore 0:
  14.8 61.5 all-gather.12
  78.9 58.8 all-gather.14
  166.7 32.3 all-gather.30
  201.4 32.3 all-gather.28
  258.0 126.1 reduce-scatter.3
  617.8 54.0 all-reduce.12
  697.7 75.7 reduce-scatter.5
  777.6 76.4 reduce-scatter.7
  857.0 34.3 all-reduce.14
  1325.2 52.2 all-gather.18
  1381.4 52.8 all-gather.16
  1437.5 52.9 all-gather.20
  1494.4 52.9 all-gather.22
  1551.1 62.5 all-gather.24
  1617.5 62.4 all-gather.26
